TPU v7x, 32 devices: a whole 2x2x4 slice. The times are simulated.
32 devices in a mesh: slab: 16 (over z, y, x), sub: 2 (over core).
Axes of the slice: x: 2, y: 2, z: 4, core: 2. Of those that a mesh axis runs over, the one named last changes fastest.
Arguments:
- velocities: float32 [3, 163840], P(None, ('slab', 'sub')), may hold values from -16 to 19
- cell_index: int32 [1, 163840], P(None, ('slab', 'sub')), may hold values from 0 to 511
- axis_choice: int32 [1, 16384], P(None, ('slab', 'sub')), may hold values from 0 to 63
- moves: int32 [1, 4, 4096], P(None, None, ('slab', 'sub')), may hold values from 0 to 5119, as said below
- shear_target: float32 [128], P('sub'), may hold values from -6 to 6
Outputs:
- velocities_final: float32 [3, 163840], P(None, ('slab', 'sub'))
- profile: float32 [16, 128], P('slab', 'sub')
Inputs may be any that keep to these rules, and one draw needn't show every extreme that they name: `moves`: in each step the 512 slots of one device's four lists are distinct.
All inputs are finite; a program needn't handle non-finite values.
Results may differ from a plain program's by a relative error of at most 0.0003.
Values sent between devices are 32-bit elements; how exact they have to be, the bound alone decides.
No kernel may reach another device: no remote copies, remote signals or barrier semaphores. Data moves between devices by JAX's collectives and lax.ppermute only.
A program may use at most 64 MiB of HBM per device.

v0:
```python
import jax
import jax.numpy as jnp
from jax import lax
from jax.sharding import PartitionSpec as P

CX = 1
CY = 64
CZ = 8
NAXES = 64
ROT_COS = -0.6427876096865393
ROT_SIN = 0.766044443118978
RESERVOIR_HEAT = 0.9
FEEDBACK = 1.0
GOLDEN = 2.399963229728653


def from_behind(block, axis, distance):
    devices = range(lax.axis_size(axis))
    route = [((i - distance) % len(devices), i) for i in devices]
    return lax.ppermute(block, axis, route)


def axis_table():
    counter = jnp.arange(NAXES, dtype=jnp.int32).astype(jnp.float32)
    height = 1.0 - (2.0 * counter + 1.0) / NAXES
    radius = jnp.sqrt(1.0 - height * height)
    return jnp.stack(
        [radius * jnp.cos(GOLDEN * counter), radius * jnp.sin(GOLDEN * counter), height]
    )


def bin_cells(values, weights, cells, totals):
    stacked = jnp.concatenate([values, weights[None, :]], 0)
    return totals.at[:, cells].add(stacked)


def cell_state(totals, choices, table):
    counts = jnp.maximum(totals[3], 1.0)
    average_value = totals[:3] / counts
    onehot = (jnp.arange(NAXES, dtype=jnp.int32)[:, None] == choices[None, :]).astype(jnp.float32)
    axes = jnp.dot(table, onehot, precision=lax.Precision.HIGHEST)
    columns = jnp.sum(totals.reshape(4, CX * CY, CZ), 2)
    block = (columns[0] / jnp.maximum(columns[3], 1.0)).reshape(CX, CY)
    return (average_value, axes, block)


def collide(relative, cells, average_value, axes, speed_multiplier, adjustment_factor):
    normal = axes[:, cells]
    cross = jnp.stack(
        [
            normal[1] * relative[2] - normal[2] * relative[1],
            normal[2] * relative[0] - normal[0] * relative[2],
            normal[0] * relative[1] - normal[1] * relative[0],
        ]
    )
    along = jnp.sum(normal * relative, 0)
    rotated = relative * ROT_COS + cross * ROT_SIN + normal * (along * (1.0 - ROT_COS))
    shifted = average_value.at[0].add(adjustment_factor)
    return shifted[:, cells] + speed_multiplier * rotated


def body(velocities, cell_index, axis_choice, moves, shear_target):
    speeds = velocities
    slabs = lax.axis_size("slab")
    sub_count = lax.axis_size("sub")
    inner_position = lax.axis_index("sub")
    count_here = speeds.shape[1]
    whole_swarm = count_here * slabs * sub_count
    width_x = CX * slabs
    block_rows = moves.shape[2]
    table = axis_table()
    slots = moves[0].reshape(-1)
    cells = cell_index[0]
    outgoing = speeds[:, slots].reshape(3, 4, block_rows)
    weights = jnp.ones((count_here,), jnp.float32)
    empty = jnp.zeros((4, CX * CY * CZ), jnp.float32)
    east_in = from_behind(outgoing[:, 1], "slab", -1)
    west_in = from_behind(outgoing[:, 0], "slab", 1)
    north_incoming = from_behind(outgoing[:, 3], "sub", -1)
    south_in = from_behind(outgoing[:, 2], "sub", 1)
    arriving = jnp.stack([east_in, west_in, north_incoming, south_in], 1).reshape(3, 4 * block_rows)
    speeds = speeds.at[:, slots].set(arriving)
    totals = bin_cells(speeds, weights, cells, empty)
    average_value, axes, profile = cell_state(totals, axis_choice[0], table)
    relative = speeds - average_value[:, cells]
    local_energy = jnp.sum(relative * relative)
    line_aggregate = jnp.sum(profile, 0)
    padded = lax.dynamic_update_slice(
        jnp.zeros((CY * sub_count,), jnp.float32), line_aggregate, (inner_position * CY,)
    )
    summed, motion_work = lax.psum((padded, local_energy), ("slab", "sub"))
    column_sum = lax.dynamic_slice(summed, (inner_position * CY,), (CY,))
    speed_multiplier = lax.rsqrt(motion_work / (3.0 * whole_swarm * RESERVOIR_HEAT) + 1e-06)
    adjustment_factor = FEEDBACK * (shear_target - column_sum / width_x)
    per_cell = jnp.broadcast_to(adjustment_factor[None, :, None], (CX, CY, CZ)).reshape(-1)
    speeds = collide(relative, cells, average_value, axes, speed_multiplier, per_cell)
    return (speeds, profile)


def solution(mesh):
    in_specs = (
        P(None, ("slab", "sub")),
        P(None, ("slab", "sub")),
        P(None, ("slab", "sub")),
        P(None, None, ("slab", "sub")),
        P("sub"),
    )
    out_specs = (P(None, ("slab", "sub")), P("slab", "sub"))
    return jax.shard_map(body, mesh=mesh, in_specs=in_specs, out_specs=out_specs, check_vma=False)
```

profile of v0, /device:TPU:0, one launch (start us, length us, event | category | flops | bytes accessed | tf_op | source)
XLA Modules:
  0.0 134.7 jit_solution(16117041994723011014)
XLA Ops:
  0.7 1.7 %copy.103 = f32[3,5120]{0,1:T(8,128)S(1)} copy(f32[3,5120]{1,0:T(4,128)} %param.7) | data formatting | bytes 122880 | tf_op args[0]
  2.4 1.0 gather_fusion
  3.4 0.1 copy.117
  3.5 0.5 collective-permute-start.3
  4.2 3.0 %collective-permute-start.1 = (f32[3,128]{1,0:T(4,128)S(1)}, f32[3,128]{1,0:T(4,128)S(1)}, u32[]{:S(2)}, u32[]{:S(2)}) collective-permute-start(f32[3,128]{1,0:T(4,128)S(1)} %bitcast.41), channel_id=1, source_target_pairs={{30,0},{0,2},{2,4},{4,6},{6,8},{8,10},{10,12},{12,14},{14,16},{16,... | collective-permute-start | bytes 4616 | tf_op jit(solution)/shard_map/ppermute | solution.py:20
  7.2 4.0 %collective-permute-start = (f32[3,128]{1,0:T(4,128)S(1)}, f32[3,128]{1,0:T(4,128)S(1)}, u32[]{:S(2)}, u32[]{:S(2)}) collective-permute-start(f32[3,128]{1,0:T(4,128)S(1)} %bitcast.42), channel_id=1, source_target_pairs={{2,0},{4,2},{6,4},{8,6},{10,8},{12,10},{14,12},{16,14},{18,16},{20... | collective-permute-start | bytes 4616 | tf_op jit(solution)/shard_map/ppermute | solution.py:20
  11.4 0.4 fusion.5
  11.8 17.7 %gather_fusion.3 = f32[5120,3]{1,0:T(8,128)} fusion(f32[3,512]{0,1:T(8,128)S(1)} %fusion.5, s32[5120]{0:T(1024)S(1)} %broadcast_clamp_fusion), kind=kCustom, calls=%fused_computation.3 | custom fusion | bytes 143360 | tf_op jit(solution)/shard_map/gather | solution.py:48
  29.4 2.5 %copy.111 = f32[5120,3]{0,1:T(4,128)S(1)} copy(f32[5120,3]{1,0:T(8,128)} %gather_fusion.3) | data formatting | bytes 122880 | tf_op jit(solution)/shard_map/gather | solution.py:48
  32.0 0.1 copy.113
  32.2 2.7 %scatter_fusion = f32[3,5120]{0,1:T(8,128)S(1)} fusion(f32[3,5120]{0,1:T(8,128)S(1)} %copy.103, s32[512]{0:T(512)S(1)} %bitcast.37, f32[512,3]{1,0:T(8,128)S(1)} %bitcast.33), kind=kCustom, calls=%fused_computation.4 | custom fusion | bytes 20480 | tf_op jit(solution)/shard_map/scatter | solution.py:82
  34.9 0.8 copy.109
  35.6 27.9 %scatter_custom_fusion.1 = f32[4,512]{0,1:T(8,128)S(1)} fusion(s32[5120]{0:T(1024)S(1)} %bitcast.35, f32[3,5120]{0,1:T(8,128)S(1)} %scatter_fusion, f32[]{:T(128)} %constant.59.clone.1, f32[]{:T(128)} %constant.55.clone.1), kind=kCustom, calls=%fused_computation.6 | custom fusion | flops 20480 | bytes 2629640 | tf_op jit(solution)/shard_map/scatter-add | solution.py:34
  63.6 0.2 fusion.3
  63.8 0.1 bitcast_reduce_fusion
  63.9 0.1 slice_divide_fusion
  64.0 13.4 %gather_fusion.2 = f32[5120,3]{1,0:T(8,128)S(1)} fusion(f32[3,512]{0,1:T(8,128)S(1)} %slice_divide_fusion, s32[5120]{0:T(1024)S(1)} %broadcast_clamp_fusion), kind=kCustom, calls=%fused_computation.2 | custom fusion | bytes 143360 | tf_op jit(solution)/shard_map/gather | solution.py:85
  77.5 0.8 copy.108
  78.3 0.1 fusion.18
  78.3 0.1 copy.118
  78.4 0.1 copy.119
  78.5 0.7 multiply_reduce_fusion.1
  79.2 0.5 bitcast_dynamic-update-slice_fusion
  79.7 38.0 %all-reduce.1 = (f32[128]{0:T(128)S(1)}, f32[]{:T(128)}) all-reduce(f32[128]{0:T(128)S(1)} %get-tuple-element.29, f32[]{:T(128)} %get-tuple-element.24), channel_id=1, replica_groups=mesh['slab'=16,'sub'=2] {'slab','sub'}, use_global_device_ids=true, to_apply=%region_3.0 | all-reduce | flops 129 | bytes 1032 | tf_op jit(solution)/shard_map/psum | solution.py:91
  117.7 0.1 multiply_subtract_fusion.4
  117.8 0.1 broadcast_in_dim.10
  117.8 0.1 broadcast_in_dim.12
  118.0 0.9 scatter-add.13
  118.9 13.4 %gather_fusion.1 = f32[5120,3]{1,0:T(8,128)S(1)} fusion(f32[3,512]{0,1:T(8,128)S(1)} %scatter-add.13, s32[5120]{0:T(1024)S(1)} %broadcast_clamp_fusion), kind=kCustom, calls=%fused_computation.1 | custom fusion | bytes 143360 | tf_op jit(solution)/shard_map/gather | solution.py:59
  132.4 0.8 copy.107
  133.8 0.1 multiply_subtract_fusion.2
  133.9 0.7 fusion.9
  (31 shorter events, 0.4 us)
Async XLA Ops:
  0.6 1.7 %copy-start.2 = (s32[1,4,128]{2,1,0:T(4,128)S(1)}, s32[1,4,128]{2,1,0:T(4,128)}, u32[]{:S(2)}) copy-start(s32[1,4,128]{2,1,0:T(4,128)} %param.10) | copy-start | bytes 6148
  0.6 10.7 %copy-start = (s32[1,5120]{1,0:T(1,128)S(1)}, s32[1,5120]{1,0:T(1,128)}, u32[]{:S(2)}) copy-start(s32[1,5120]{1,0:T(1,128)} %param.8) | copy-start | bytes 61444
  0.7 10.7 %copy-start.1 = (s32[1,512]{1,0:T(1,128)S(1)}, s32[1,512]{1,0:T(1,128)}, u32[]{:S(2)}) copy-start(s32[1,512]{1,0:T(1,128)} %param.9) | copy-start | bytes 6148
  3.5 28.4 %collective-permute-start.3 = (f32[3,128]{1,0:T(4,128)S(1)}, f32[3,128]{1,0:T(4,128)S(1)}, u32[]{:S(2)}, u32[]{:S(2)}) collective-permute-start(f32[3,128]{1,0:T(4,128)S(1)} %bitcast.39), channel_id=1, source_target_pairs={{1,0},{0,1},{3,2},{2,3},{5,4},{4,5},{7,6},{6,7},{9,8},{8,9},{11,10... | collective-permute-start | bytes 4616 | tf_op jit(solution)/shard_map/ppermute | solution.py:20
  4.1 27.9 %collective-permute-start.2 = (f32[3,128]{1,0:T(4,128)S(1)}, f32[3,128]{1,0:T(4,128)S(1)}, u32[]{:S(2)}, u32[]{:S(2)}) collective-permute-start(f32[3,128]{1,0:T(4,128)S(1)} %bitcast.40), channel_id=1, source_target_pairs={{1,0},{0,1},{3,2},{2,3},{5,4},{4,5},{7,6},{6,7},{9,8},{8,9},{11,10... | collective-permute-start | bytes 4616 | tf_op jit(solution)/shard_map/ppermute | solution.py:20
  4.2 27.8 %collective-permute-start.1 = (f32[3,128]{1,0:T(4,128)S(1)}, f32[3,128]{1,0:T(4,128)S(1)}, u32[]{:S(2)}, u32[]{:S(2)}) collective-permute-start(f32[3,128]{1,0:T(4,128)S(1)} %bitcast.41), channel_id=1, source_target_pairs={{30,0},{0,2},{2,4},{4,6},{6,8},{8,10},{10,12},{12,14},{14,16},{16,... | collective-permute-start | bytes 4616 | tf_op jit(solution)/shard_map/ppermute | solution.py:20
  7.2 24.8 %collective-permute-start = (f32[3,128]{1,0:T(4,128)S(1)}, f32[3,128]{1,0:T(4,128)S(1)}, u32[]{:S(2)}, u32[]{:S(2)}) collective-permute-start(f32[3,128]{1,0:T(4,128)S(1)} %bitcast.42), channel_id=1, source_target_pairs={{2,0},{4,2},{6,4},{8,6},{10,8},{12,10},{14,12},{16,14},{18,16},{20... | collective-permute-start | bytes 4616 | tf_op jit(solution)/shard_map/ppermute | solution.py:20
  63.6 54.1 %copy-start.3 = (f32[64]{0:T(128)S(1)}, f32[64]{0:T(128)}, u32[]{:S(2)}) copy-start(f32[64]{0:T(128)} %param.11) | copy-start | bytes 772
where the time goes:
time: 135 us
  local copies, waits for them, and re-layouts  56.5 us (42%)
  blocking collectives  38 us (28%)
  other arithmetic  30.7 us (23%)
  starting transfers between devices  7.57 us (6%)
  between operations  1.62 us (1%)
    psum x1, blocking collectives, body(): summed, motion_work = lax.psum((padded, local_energy), ('slab', 'sub'))  38 us
    scatter-add x1, other arithmetic, bin_cells(): return totals.at[:, cells].add(stacked)  27.9 us
    gather x2, local copies, waits for them, and re-layouts, collide(): normal = axes[:, cells]  20.2 us
    gather x2, local copies, waits for them, and re-layouts, body(): relative = speeds - average_value[:, cells]  14.2 us
    gather x2, local copies, waits for them, and re-layouts, collide(): return shifted[:, cells] + speed_multiplier * rotated  14.2 us
    ppermute x4, starting transfers between devices, from_behind(): return lax.ppermute(block, axis, route)  7.57 us
    scatter x2, local copies, waits for them, and re-layouts, body(): speeds = speeds.at[:, slots].set(arriving)  3.44 us
  transfers between devices with their start and end apart: 4, of which 0 were waited for; matrix products, arithmetic and copies ran while one was open for 15% of the time, Pallas kernels for 0%

commit v1 on v0

--- a/solution.py
+++ b/solution.py
@@ -88,7 +88,7 @@
     padded = lax.dynamic_update_slice(
         jnp.zeros((CY * sub_count,), jnp.float32), line_aggregate, (inner_position * CY,)
     )
-    summed, motion_work = lax.psum((padded, local_energy), ("slab", "sub"))
+    summed, motion_work = lax.psum(lax.psum((padded, local_energy), "sub"), "slab")
     column_sum = lax.dynamic_slice(summed, (inner_position * CY,), (CY,))
     speed_multiplier = lax.rsqrt(motion_work / (3.0 * whole_swarm * RESERVOIR_HEAT) + 1e-06)
     adjustment_factor = FEEDBACK * (shear_target - column_sum / width_x)

time: 135 us -> 139 us (1.030)
  blocking collectives: 38 us -> 42.3 us
    psum x1 -> x2, blocking collectives: 38 us -> 42.3 us  [the longest x1 39.2 us: body(): lax.psum(lax.psum((padded, local_energy), 'sub'), 'slab')]
where the time goes in v1:
time: 139 us
  local copies, waits for them, and re-layouts  56.5 us (41%)
  blocking collectives  42.3 us (30%)
  other arithmetic  30.7 us (22%)
  starting transfers between devices  7.57 us (5%)
  between operations  1.62 us (1%)
    psum x1, blocking collectives, body(): lax.psum(lax.psum((padded, local_energy), 'sub'), 'slab')  39.2 us
    scatter-add x1, other arithmetic, bin_cells(): return totals.at[:, cells].add(stacked)  27.9 us
    gather x2, local copies, waits for them, and re-layouts, collide(): normal = axes[:, cells]  20.2 us
    gather x2, local copies, waits for them, and re-layouts, body(): relative = speeds - average_value[:, cells]  14.2 us
    gather x2, local copies, waits for them, and re-layouts, collide(): return shifted[:, cells] + speed_multiplier * rotated  14.2 us
    ppermute x4, starting transfers between devices, from_behind(): return lax.ppermute(block, axis, route)  7.57 us
    scatter x2, local copies, waits for them, and re-layouts, body(): speeds = speeds.at[:, slots].set(arriving)  3.44 us
    psum x1, blocking collectives, body(): lax.psum((padded, local_energy), 'sub')  3.08 us
  transfers between devices with their start and end apart: 4, of which 0 were waited for; matrix products, arithmetic and copies ran while one was open for 15% of the time, Pallas kernels for 0%

profile of v1, /device:TPU:0, one launch (start us, length us, event | category | flops | bytes accessed | tf_op | source)
XLA Modules:
  0.0 139.0 jit_solution(18188697162355460351)
XLA Ops:
  0.7 1.7 %copy.103 = f32[3,5120]{0,1:T(8,128)S(1)} copy(f32[3,5120]{1,0:T(4,128)} %param.7) | data formatting | bytes 122880 | tf_op args[0]
  2.4 1.0 gather_fusion
  3.5 0.5 collective-permute-start.3
  4.2 3.0 %collective-permute-start.1 = (f32[3,128]{1,0:T(4,128)S(1)}, f32[3,128]{1,0:T(4,128)S(1)}, u32[]{:S(2)}, u32[]{:S(2)}) collective-permute-start(f32[3,128]{1,0:T(4,128)S(1)} %bitcast.41), channel_id=1, source_target_pairs={{30,0},{0,2},{2,4},{4,6},{6,8},{8,10},{10,12},{12,14},{14,16},{16,... | collective-permute-start | bytes 4616 | tf_op jit(solution)/shard_map/ppermute | solution.py:20
  7.2 4.0 %collective-permute-start = (f32[3,128]{1,0:T(4,128)S(1)}, f32[3,128]{1,0:T(4,128)S(1)}, u32[]{:S(2)}, u32[]{:S(2)}) collective-permute-start(f32[3,128]{1,0:T(4,128)S(1)} %bitcast.42), channel_id=1, source_target_pairs={{2,0},{4,2},{6,4},{8,6},{10,8},{12,10},{14,12},{16,14},{18,16},{20... | collective-permute-start | bytes 4616 | tf_op jit(solution)/shard_map/ppermute | solution.py:20
  11.4 0.4 fusion.5
  11.8 17.7 %gather_fusion.3 = f32[5120,3]{1,0:T(8,128)} fusion(f32[3,512]{0,1:T(8,128)S(1)} %fusion.5, s32[5120]{0:T(1024)S(1)} %broadcast_clamp_fusion), kind=kCustom, calls=%fused_computation.3 | custom fusion | bytes 143360 | tf_op jit(solution)/shard_map/gather | solution.py:48
  29.4 2.5 %copy.111 = f32[5120,3]{0,1:T(4,128)S(1)} copy(f32[5120,3]{1,0:T(8,128)} %gather_fusion.3) | data formatting | bytes 122880 | tf_op jit(solution)/shard_map/gather | solution.py:48
  32.0 0.1 copy.113
  32.2 2.7 %scatter_fusion = f32[3,5120]{0,1:T(8,128)S(1)} fusion(f32[3,5120]{0,1:T(8,128)S(1)} %copy.103, s32[512]{0:T(512)S(1)} %bitcast.37, f32[512,3]{1,0:T(8,128)S(1)} %bitcast.33), kind=kCustom, calls=%fused_computation.4 | custom fusion | bytes 20480 | tf_op jit(solution)/shard_map/scatter | solution.py:82
  34.9 0.8 copy.109
  35.6 27.9 %scatter_custom_fusion.1 = f32[4,512]{0,1:T(8,128)S(1)} fusion(s32[5120]{0:T(1024)S(1)} %bitcast.35, f32[3,5120]{0,1:T(8,128)S(1)} %scatter_fusion, f32[]{:T(128)} %constant.59.clone.1, f32[]{:T(128)} %constant.55.clone.1), kind=kCustom, calls=%fused_computation.6 | custom fusion | flops 20480 | bytes 2629640 | tf_op jit(solution)/shard_map/scatter-add | solution.py:34
  63.6 0.2 fusion.3
  63.8 0.1 bitcast_reduce_fusion
  63.9 0.1 slice_divide_fusion
  64.0 13.4 %gather_fusion.2 = f32[5120,3]{1,0:T(8,128)S(1)} fusion(f32[3,512]{0,1:T(8,128)S(1)} %slice_divide_fusion, s32[5120]{0:T(1024)S(1)} %broadcast_clamp_fusion), kind=kCustom, calls=%fused_computation.2 | custom fusion | bytes 143360 | tf_op jit(solution)/shard_map/gather | solution.py:85
  77.5 0.8 copy.108
  78.3 0.1 fusion.18
  78.3 0.1 copy.118
  78.4 0.1 copy.119
  78.5 0.7 multiply_reduce_fusion.1
  79.2 0.5 bitcast_dynamic-update-slice_fusion
  79.7 3.1 %all-reduce.2 = (f32[128]{0:T(128)S(1)}, f32[]{:T(128)}) all-reduce(f32[128]{0:T(128)S(1)} %get-tuple-element.31, f32[]{:T(128)} %get-tuple-element.24), channel_id=1, replica_groups=mesh['slab'=16,'sub'=2] {'sub'}, use_global_device_ids=true, to_apply=%region_3.0 | all-reduce | flops 129 | bytes 1032 | tf_op jit(solution)/shard_map/psum | solution.py:91
  82.8 39.2 %all-reduce.1 = (f32[128]{0:T(128)S(1)}, f32[]{:T(128)}) all-reduce(f32[128]{0:T(128)S(1)} %get-tuple-element.28, f32[]{:T(128)} %get-tuple-element.29), channel_id=1, replica_groups=mesh['slab'=16,'sub'=2] {'slab'}, use_global_device_ids=true, to_apply=%region_4.0 | all-reduce | flops 129 | bytes 1032 | tf_op jit(solution)/shard_map/psum | solution.py:91
  122.0 0.1 multiply_subtract_fusion.4
  122.1 0.1 broadcast_in_dim.10
  122.1 0.1 broadcast_in_dim.12
  122.3 0.9 scatter-add.13
  123.2 13.4 %gather_fusion.1 = f32[5120,3]{1,0:T(8,128)S(1)} fusion(f32[3,512]{0,1:T(8,128)S(1)} %scatter-add.13, s32[5120]{0:T(1024)S(1)} %broadcast_clamp_fusion), kind=kCustom, calls=%fused_computation.1 | custom fusion | bytes 143360 | tf_op jit(solution)/shard_map/gather | solution.py:59
  136.7 0.8 copy.107
  138.1 0.1 multiply_subtract_fusion.2
  138.2 0.7 fusion.9
  (32 shorter events, 0.5 us)
Async XLA Ops:
  0.6 1.7 %copy-start.2 = (s32[1,4,128]{2,1,0:T(4,128)S(1)}, s32[1,4,128]{2,1,0:T(4,128)}, u32[]{:S(2)}) copy-start(s32[1,4,128]{2,1,0:T(4,128)} %param.10) | copy-start | bytes 6148
  0.6 10.7 %copy-start = (s32[1,5120]{1,0:T(1,128)S(1)}, s32[1,5120]{1,0:T(1,128)}, u32[]{:S(2)}) copy-start(s32[1,5120]{1,0:T(1,128)} %param.8) | copy-start | bytes 61444
  0.7 10.7 %copy-start.1 = (s32[1,512]{1,0:T(1,128)S(1)}, s32[1,512]{1,0:T(1,128)}, u32[]{:S(2)}) copy-start(s32[1,512]{1,0:T(1,128)} %param.9) | copy-start | bytes 6148
  3.5 28.4 %collective-permute-start.3 = (f32[3,128]{1,0:T(4,128)S(1)}, f32[3,128]{1,0:T(4,128)S(1)}, u32[]{:S(2)}, u32[]{:S(2)}) collective-permute-start(f32[3,128]{1,0:T(4,128)S(1)} %bitcast.39), channel_id=1, source_target_pairs={{1,0},{0,1},{3,2},{2,3},{5,4},{4,5},{7,6},{6,7},{9,8},{8,9},{11,10... | collective-permute-start | bytes 4616 | tf_op jit(solution)/shard_map/ppermute | solution.py:20
  4.1 27.9 %collective-permute-start.2 = (f32[3,128]{1,0:T(4,128)S(1)}, f32[3,128]{1,0:T(4,128)S(1)}, u32[]{:S(2)}, u32[]{:S(2)}) collective-permute-start(f32[3,128]{1,0:T(4,128)S(1)} %bitcast.40), channel_id=1, source_target_pairs={{1,0},{0,1},{3,2},{2,3},{5,4},{4,5},{7,6},{6,7},{9,8},{8,9},{11,10... | collective-permute-start | bytes 4616 | tf_op jit(solution)/shard_map/ppermute | solution.py:20
  4.2 27.8 %collective-permute-start.1 = (f32[3,128]{1,0:T(4,128)S(1)}, f32[3,128]{1,0:T(4,128)S(1)}, u32[]{:S(2)}, u32[]{:S(2)}) collective-permute-start(f32[3,128]{1,0:T(4,128)S(1)} %bitcast.41), channel_id=1, source_target_pairs={{30,0},{0,2},{2,4},{4,6},{6,8},{8,10},{10,12},{12,14},{14,16},{16,... | collective-permute-start | bytes 4616 | tf_op jit(solution)/shard_map/ppermute | solution.py:20
  7.2 24.8 %collective-permute-start = (f32[3,128]{1,0:T(4,128)S(1)}, f32[3,128]{1,0:T(4,128)S(1)}, u32[]{:S(2)}, u32[]{:S(2)}) collective-permute-start(f32[3,128]{1,0:T(4,128)S(1)} %bitcast.42), channel_id=1, source_target_pairs={{2,0},{4,2},{6,4},{8,6},{10,8},{12,10},{14,12},{16,14},{18,16},{20... | collective-permute-start | bytes 4616 | tf_op jit(solution)/shard_map/ppermute | solution.py:20
  63.6 58.4 %copy-start.3 = (f32[64]{0:T(128)S(1)}, f32[64]{0:T(128)}, u32[]{:S(2)}) copy-start(f32[64]{0:T(128)} %param.11) | copy-start | bytes 772
